TPU v7x, 512 devices: a whole 4x4x16 slice. The times are simulated.
512 devices in a mesh: cells: 128 (over z, y, core), mem: 4 (over x).
Axes of the slice: x: 4, y: 4, z: 16, core: 2. Of those that a mesh axis runs over, the one named last changes fastest.
Arguments:
- ensemble: float32 [512, 262144], P('mem', 'cells'), may hold values from -6 to 6
- observed: float32 [262144], P('cells'), may hold values from -6 to 6
- obs_sigma: float32 [262144], P('cells'), may hold values from 0.1 to 1
- obs_index: int32 [262144], P('cells'), may hold values from 0 to 2047
- member_seeds: int32 [512], P('mem'), may hold values from 1 to 65520
Outputs:
- updated: float32 [512, 262144], P('mem', 'cells')
All inputs are finite; a program needn't handle non-finite values.
Results may differ from a plain program's by a relative error of at most 0.0003.
Values sent between devices are 32-bit elements; how exact they have to be, the bound alone decides.
A program may use at most 64 MiB of HBM per device.

v0:
```python
import math
import jax
import jax.numpy as jnp
from jax import lax
from jax.sharding import Mesh
from jax.sharding import PartitionSpec as P

SECTION = 1
CELLS = ("cells_0", "cells_1", "cells_2")
plan = (28.0 / 3.0, 7.0, 4.0, 2.0)


def from_everyone(shard, axis):
    copies = jnp.broadcast_to(shard, (lax.axis_size(axis), *shard.shape))
    return lax.all_to_all(copies, axis, split_axis=0, concat_axis=0, tiled=True)


def over_copies(shard, axis):
    return from_everyone(shard, axis).sum(axis=0)


def together(arrays, axis):
    ends = [0]
    for a in arrays:
        ends.append(ends[-1] + a.size)
    total = over_copies(jnp.concatenate([a.ravel() for a in arrays]), axis)
    return tuple((total[b:e].reshape(a.shape) for a, b, e in zip(arrays, ends, ends[1:])))


def rows_for(lines, devices):
    spare = -len(lines) % devices
    return jnp.pad(lines, [(0, spare)] + [(0, 0)] * (lines.ndim - 1))


def laid_out(tiles, dim):
    tiles = jnp.moveaxis(tiles, 0, dim)
    lengths = tiles.shape
    return tiles.reshape(*lengths[:dim], lengths[dim] * lengths[dim + 1], *lengths[dim + 2 :])


def gather_axes(shard, axes, dim):
    far, near = axes
    leading = from_everyone(shard, far)
    tiles = jnp.swapaxes(from_everyone(leading, near), 0, 1)
    return laid_out(tiles.reshape(-1, *shard.shape), dim)


def in_blocks(shard, dim, devices):
    lengths = shard.shape
    tiles = shard.reshape(*lengths[:dim], devices, lengths[dim] // devices, *lengths[dim + 1 :])
    return jnp.moveaxis(tiles, dim, 0)


def summed_on_arrival(shard, axis, dim):
    devices = lax.axis_size(axis)
    tiles = lax.all_to_all(in_blocks(shard, dim, devices), axis, 0, 0, tiled=True)
    return jnp.sum(tiles, axis=0)


def summed_rows(shard, axes, dim):
    far, near = axes
    tiles = in_blocks(shard, dim, lax.axis_size(far))
    nearer = summed_on_arrival(tiles, near, dim + 1)
    arrived = lax.all_to_all(nearer, far, split_axis=0, concat_axis=0, tiled=True)
    return arrived.sum(axis=0)


def nested_sum(shard, axes):
    padded = rows_for(shard, lax.axis_size(axes[0]) * lax.axis_size(axes[1]))
    whole = gather_axes(summed_rows(padded, axes, 0), axes, 0)
    return lax.slice_in_dim(whole, 0, len(shard)).reshape(shard.shape)


def together_2(arrays, axis):
    ends = [0]
    for a in arrays:
        ends.append(ends[-1] + a.size)
    total = nested_sum(jnp.concatenate([a.ravel() for a in arrays]), axis)
    return tuple((total[b:e].reshape(a.shape) for a, b, e in zip(arrays, ends, ends[1:])))


def perturbation(member_seeds, positions):
    seeds_col = member_seeds[:, None]
    where_row = positions[None, :]
    hashed = (seeds_col * 389 % 65521 + where_row % 65521 * (seeds_col % 997 + 1)) % 65521
    return math.sqrt(2.0) * jnp.cos(2.0 * math.pi / 65521.0 * hashed.astype(jnp.float32))


def shards(ensemble, observed, obs_sigma, obs_index, member_seeds):
    highest = lax.Precision.HIGHEST
    own_members, cell_count = ensemble.shape
    obs_count = observed.shape[0]
    members = own_members * lax.axis_size("mem")
    alpha = jnp.float32(plan[SECTION])
    value = ensemble[:, obs_index]
    predicted = jnp.tanh(value) + 0.5 * value
    totals = together((jnp.sum(ensemble, axis=0), jnp.sum(predicted, axis=0)), "mem")
    mean_state = totals[0] / members
    mean_pred = totals[1] / members
    positions = lax.axis_index(CELLS) * obs_count + jnp.arange(obs_count, dtype=jnp.int32)
    noise = perturbation(member_seeds, positions)
    scaled = (predicted - mean_pred) / (obs_sigma * math.sqrt(members - 1.0))
    innovation = observed / obs_sigma + jnp.sqrt(alpha) * noise - predicted / obs_sigma
    gathered = lax.all_gather(scaled, "mem", axis=0, tiled=True)
    gram_matrix, cross_terms = together_2(
        (
            jnp.dot(gathered, gathered.T, precision=highest),
            jnp.dot(gathered, innovation.T, precision=highest),
        ),
        (("cells_0", "cells_1"), "cells_2"),
    )
    factor = jnp.linalg.cholesky(gram_matrix + alpha * jnp.eye(members, dtype=jnp.float32))
    weights = jax.scipy.linalg.cho_solve((factor, True), cross_terms)
    anomalies = ensemble - mean_state
    change = jnp.zeros((own_members, cell_count), jnp.float32) + jnp.dot(
        weights.T, lax.all_gather(anomalies, "mem", axis=0, tiled=True), precision=highest
    )
    return ensemble + change / math.sqrt(members - 1.0)


def solution(mesh):
    finer = Mesh(
        mesh.devices.reshape(16, 4, 2, mesh.shape["mem"]), ("cells_0", "cells_1", "cells_2", "mem")
    )
    placed = (P("mem", CELLS), P(CELLS), P(CELLS), P(CELLS), P("mem"))
    return jax.shard_map(
        shards, mesh=finer, in_specs=placed, out_specs=P("mem", CELLS), check_vma=False
    )
```

profile of v0, /device:TPU:1, one launch (start us, length us, event | category | flops | bytes accessed | tf_op | source)
XLA Modules:
  0.0 412.3 jit_solution(3694493013845789510)
XLA Ops:
  6.5 1.6 copy.68
  8.1 5.5 %gather_fusion = f32[2048,128]{1,0:T(8,128)S(1)} fusion(f32[128,2048]{0,1:T(8,128)S(1)} %copy.68, s32[2048]{0:T(1024)S(1)} %fusion.75), kind=kCustom, calls=%fused_computation | custom fusion | bytes 2105344 | tf_op jit(solution)/shard_map/gather | solution.py:95
  14.0 0.8 copy-done.1
  15.0 9.1 %all_to_all.34 = f32[4,1,4096]{2,1,0:T(1,128)S(1)} all-to-all(f32[4,1,4096]{2,1,0:T(1,128)S(1)} %broadcast_in_dim.10), channel_id=1, replica_groups=mesh['cells_0'=16,'cells_1'=4,'cells_2'=2,'mem'=4] {'mem'}, dimensions={0} | all-to-all | bytes 131072 | tf_op jit(solution)/shard_map/all_to_all | solution.py:15
  24.2 1.5 divide_bitcast_fusion
  25.8 61.8 %all-gather.3.cloned.1.call-done = f32[512,2048]{0,1:T(8,128)} async-done(((f32[128,2048]{0,1:T(8,128)}), f32[512,2048]{0,1:T(8,128)}) %all-gather.3.cloned.1.call-update) | async-done | bytes 4194320 | tf_op jit(solution)/shard_map/all_gather | solution.py:104
  87.6 10.6 %convolution_bitcast_fusion.1 = f32[64,4,8,128]{3,2,1,0:T(8,128)S(1)} fusion(f32[512,2048]{0,1:T(8,128)} %all-gather.3.cloned.1.call-done), kind=kOutput, calls=%fused_computation.7 | convolution fusion | flops 6442450944 | bytes 5242880 | tf_op jit(solution)/shard_map/dot_general | solution.py:107
  98.4 10.8 %convolution_bitcast_fusion = f32[65536]{0:T(1024)S(1)} fusion(f32[512,2048]{0,1:T(8,128)S(1)} %copy-done, f32[2048,128]{1,0:T(8,128)S(1)} %gather_fusion, f32[2048]{0:T(1024)S(1)} %copy-done.6, s32[128]{0:T(128)S(1)} %get-tuple-element.58, s32[2048]{0:T(1024)S(1)} %add_select_fusion.1, s32[128]{0:T(128)S(1)} %get-tuple-element.57, ...), kind=kOutput, calls=%fused_computation.3 | convolution fusion | flops 1614807040 | bytes 5530624 | tf_op jit(solution)/shard_map/dot_general | solution.py:108
  109.3 1.8 reshape_reshape.4
  111.0 1.6 copy.70
  112.6 6.9 %all_to_all.35 = f32[2,64,2560]{2,1,0:T(8,128)S(1)} all-to-all(f32[2,64,2560]{2,1,0:T(8,128)S(1)} %copy.70), channel_id=1, replica_groups=mesh['cells_0'=16,'cells_1'=4,'cells_2'=2,'mem'=4] {'cells_2'}, dimensions={0} | all-to-all | bytes 2621440 | tf_op jit(solution)/shard_map/all_to_all | solution.py:56
  120.1 51.1 %all_to_all.36 = f32[64,1,2560]{2,1,0:T(1,128)S(1)} all-to-all(f32[64,1,2560]{2,1,0:T(1,128)S(1)} %all_to_all.24), channel_id=1, replica_groups=mesh['cells_0'=16,'cells_1'=4,'cells_2'=2,'mem'=4] {'cells_0','cells_1'}, dimensions={0} | all-to-all | bytes 1310720 | tf_op jit(solution)/shard_map/all_to_all | solution.py:64
  171.6 1.2 broadcast_in_dim.12
  172.8 7.9 %all-to-all-start.3 = ((f32[64,1,2560]{2,1,0:T(1,128)}), f32[64,1,2560]{2,1,0:T(1,128)S(1)}, u32[]{:S(2)}, u32[]{:S(2)}) async-start(f32[64,1,2560]{2,1,0:T(1,128)} %broadcast_in_dim.12), calls=%async_computation.3 | async-start | bytes 1310720 | tf_op jit(solution)/shard_map/all_to_all | solution.py:15
  180.7 1.1 broadcast_subtract_fusion
  181.9 33.7 %all-to-all-done.3 = f32[64,1,2560]{2,1,0:T(1,128)S(1)} async-done(((f32[64,1,2560]{2,1,0:T(1,128)}), f32[64,1,2560]{2,1,0:T(1,128)S(1)}, u32[]{:S(2)}, u32[]{:S(2)}) %all-to-all-start.3) | async-done | bytes 655392 | tf_op jit(solution)/shard_map/all_to_all | solution.py:15
  215.7 8.9 %all_to_all.37 = f32[2,64,2560]{2,1,0:T(8,128)S(1)} all-to-all(f32[2,64,2560]{2,1,0:T(8,128)S(1)} %broadcast_in_dim.24), channel_id=1, replica_groups=mesh['cells_0'=16,'cells_1'=4,'cells_2'=2,'mem'=4] {'cells_2'}, dimensions={0} | all-to-all | bytes 2621440 | tf_op jit(solution)/shard_map/all_to_all | solution.py:15
  224.7 1.0 copy.71
  225.7 2.1 slice.179
  227.8 2.3 slice.197
  230.1 1.6 copy.89
  231.7 1.1 select_add_fusion
  232.8 2.6 copy.73
  235.3 1.4 fusion.8
  236.8 1.0 copy-done.2
  237.8 11.7 %cholesky.103 = f32[128,128]{1,0:T(8,128)S(1)} custom-call(f32[128,128]{1,0:T(8,128)S(1)} %cholesky.263), custom_call_target="Cholesky" | custom-call | tf_op jit(solution)/shard_map/jit(cholesky)/cholesky | solution.py:112
  249.6 9.8 %custom-call.34 = f32[1,128,128]{1,2,0:T(8,128)S(1)} custom-call(f32[1,128,128]{2,1,0:T(8,128)S(1)} %get-tuple-element.52), custom_call_target="InvertDiagBlocksLowerTriangular" | custom-call | tf_op jit(solution)/shard_map/jit(cholesky)/cholesky | solution.py:112
  259.4 1.2 fusion.37
  260.6 1.3 convolution_subtract_fusion
  261.9 0.7 copy-done.3
  262.6 11.8 %cholesky.215 = f32[128,128]{1,0:T(8,128)S(1)} custom-call(f32[128,128]{1,0:T(8,128)S(1)} %cholesky.267), custom_call_target="Cholesky" | custom-call | tf_op jit(solution)/shard_map/jit(cholesky)/cholesky | solution.py:112
  274.4 0.6 select_reduce_fusion.2
  275.1 0.8 copy.75
  276.2 10.6 %custom-call.35 = f32[1,128,128]{1,2,0:T(8,128)S(1)} custom-call(f32[1,128,128]{2,1,0:T(8,128)} %get-tuple-element.50), custom_call_target="InvertDiagBlocksLowerTriangular" | custom-call | tf_op jit(solution)/shard_map/jit(cholesky)/cholesky | solution.py:112
  286.8 0.9 constant_dynamic-update-slice_fusion.3
  287.8 1.2 convolution_dynamic-update-slice_fusion
  289.0 1.5 convolution_subtract_fusion.1
  290.5 0.6 cholesky.272
  291.2 13.2 %cholesky.236 = f32[128,128]{1,0:T(8,128)} custom-call(f32[128,128]{1,0:T(8,128)} %cholesky.272), custom_call_target="Cholesky" | custom-call | tf_op jit(solution)/shard_map/jit(cholesky)/cholesky | solution.py:112
  304.3 1.5 select_reduce_fusion.1
  305.8 1.6 copy.78
  307.4 0.8 constant_dynamic-update-slice_fusion
  308.2 11.3 %custom-call.36 = f32[1,128,128]{1,2,0:T(8,128)} custom-call(f32[1,128,128]{2,1,0:T(8,128)} %get-tuple-element.48), custom_call_target="InvertDiagBlocksLowerTriangular" | custom-call | tf_op jit(solution)/shard_map/jit(cholesky)/cholesky | solution.py:112
  319.5 1.1 convolution_dynamic-update-slice_fusion.1
  320.6 2.1 slice.181
  322.7 1.5 convolution_subtract_fusion.8
  324.3 11.7 %cholesky.253 = f32[128,128]{1,0:T(8,128)S(1)} custom-call(f32[128,128]{1,0:T(8,128)S(1)} %convolution_subtract_fusion.8), custom_call_target="Cholesky" | custom-call | tf_op jit(solution)/shard_map/jit(cholesky)/cholesky | solution.py:112
  336.1 0.7 compare_reduce_fusion.2
  339.8 0.6 compare_reduce_fusion
  341.1 10.8 %while.1 = (s32[]{:T(128)}, f32[512,512]{0,1:T(8,128)S(1)}, s32[4,2]{0,1:T(2,128)S(1)}, f32[4,128,128]{2,1,0:T(8,128)}, s32[]{:T(128)}) while((s32[]{:T(128)}, f32[512,512]{0,1:T(8,128)S(1)}, s32[4,2]{0,1:T(2,128)S(1)}, f32[4,128,128]{2,1,0:T(8,128)}, s32[]{:T(128)}) %tuple.33), condition=%wide.while_cond, body=%wide.while_body.sunk | while | flops 2 | bytes 393829 | solution.py:113
  341.8 1.3 dynamic-slice.7
  343.2 0.6 bitcast_dynamic-update-slice_fusion.2
  344.5 1.3 dynamic-slice.7
  345.9 0.6 bitcast_dynamic-update-slice_fusion.2
  347.2 1.3 dynamic-slice.7
  348.6 0.6 bitcast_dynamic-update-slice_fusion.2
  349.9 1.3 dynamic-slice.7
  351.3 0.6 bitcast_dynamic-update-slice_fusion.2
  351.9 40.4 %custom-call.37 = f32[4,128,128]{1,2,0:T(8,128)S(1)} custom-call(f32[4,128,128]{2,1,0:T(8,128)} %get-tuple-element.12), custom_call_target="InvertDiagBlocksLowerTriangular" | custom-call | tf_op jit(solution)/shard_map/jit(_cho_solve)/triangular_solve | solution.py:113
  392.3 1.1 fusion.61
  393.4 1.1 convolution_subtract_fusion.5
  394.8 1.2 convolution_subtract_fusion.4
  396.4 1.3 convolution_subtract_fusion.7
  399.7 5.5 %fusion = f32[128,2048]{1,0:T(8,128)} fusion(f32[128,2048]{1,0:T(8,128)S(1)} %copy-done.1, f32[512,2048]{1,0:T(8,128)} %all-gather.5.cloned.1.call-done, f32[128,128]{1,0:T(8,128)S(1)} %fusion.73, f32[128,128]{1,0:T(8,128)S(1)} %fusion.71, f32[128,128]{1,0:T(8,128)S(1)} %fusion.69, f32[128,128]{1,0:T(8,128)S(1)} %fusion.68), kind=kOutput, calls=%fused_computation.5 | convolution fusion | flops 1611333632 | bytes 6553600 | tf_op jit(solution)/shard_map/dot_general | solution.py:115
  (72 shorter events, 9.5 us)
Async XLA Ops:
  6.5 1.6 copy-start.4
  6.5 81.0 %all-gather.3.cloned.1.call-start = ((), (), s32[]{:S(2)}) async-start(), calls=%async_computation.5 | async-start | bytes 5242880 | tf_op jit(solution)/shard_map/all_gather | solution.py:104
  13.6 1.2 copy-start.1
  13.6 10.5 %copy-start.5 = (f32[2048]{0:T(1024)S(1)}, f32[2048]{0:T(1024)}, u32[]{:S(2)}) copy-start(f32[2048]{0:T(1024)} %param.6) | copy-start | bytes 24580
  13.6 10.5 %copy-start.6 = (f32[2048]{0:T(1024)S(1)}, f32[2048]{0:T(1024)}, u32[]{:S(2)}) copy-start(f32[2048]{0:T(1024)} %param.7) | copy-start | bytes 24580
  24.2 1.6 copy-start.7
  87.6 10.9 %copy-start = (f32[512,2048]{0,1:T(8,128)S(1)}, f32[512,2048]{0,1:T(8,128)}, u32[]{:S(2)}) copy-start(f32[512,2048]{0,1:T(8,128)} %all-gather.3.cloned.1.call-done) | copy-start | bytes 12582916
  172.8 42.8 %all-to-all-start.3 = ((f32[64,1,2560]{2,1,0:T(1,128)}), f32[64,1,2560]{2,1,0:T(1,128)S(1)}, u32[]{:S(2)}, u32[]{:S(2)}) async-start(f32[64,1,2560]{2,1,0:T(1,128)} %broadcast_in_dim.12), calls=%async_computation.3 | async-start | bytes 1310720 | tf_op jit(solution)/shard_map/all_to_all | solution.py:15
  180.7 219.0 %all-gather.5.cloned.1.call-start = ((), (), s32[]{:S(2)}) async-start(), calls=%async_computation.6 | async-start | bytes 5242880 | tf_op jit(solution)/shard_map/all_gather | solution.py:116
  236.8 1.0 copy-start.2
  261.9 0.7 copy-start.3
Sparse Core Ops, SparseCore 0:
  25.8 61.6 all-gather.2
  183.6 56.8 all-gather.4
where the time goes:
time: 418 us; the launch traced here: 412 us
  other arithmetic  132 us (32%)
  waiting for transfers between devices  95.6 us (23%)
  blocking collectives  76 us (18%)
  local copies, waits for them, and re-layouts  42.6 us (10%)
  matrix products  41.9 us (10%)
  between operations  16.5 us (4%)
  starting transfers between devices  7.93 us (2%)
    another operation x15, other arithmetic, shards(): jnp.linalg.cholesky(gram_matrix + alpha * jnp.eye(members, dtype=jnp.floa...  84.9 us
    all_gather x1, waiting for transfers between devices, shards(): gathered = lax.all_gather(scaled, 'mem', axis=0, tiled=True)  61.8 us
    all_to_all x1, blocking collectives, summed_rows(): lax.all_to_all(nearer, far, split_axis=0, concat_axis=0, tiled=True)  51.1 us
    another operation x3, other arithmetic, shards(): weights = jax.scipy.linalg.cho_solve((factor, True), cross_terms)  40.5 us
    all_to_all x1, waiting for transfers between devices, from_everyone(): return lax.all_to_all(copies, axis, split_axis=0, concat_axis=0, tiled=True)  33.7 us
    all_to_all x2, blocking collectives, from_everyone(): return lax.all_to_all(copies, axis, split_axis=0, concat_axis=0, tiled=True)  18 us
    dot_general x1, matrix products, shards(): jnp.dot(gathered, innovation.T, precision=highest)  10.8 us
    another operation x20, local copies, waits for them, and re-layouts  10.7 us
  transfers between devices with their start and end apart: 3, of which 2 were waited for; matrix products, arithmetic and copies ran while one was open for 42% of the time, Pallas kernels for 0%

commit v1 on v0

--- a/solution.py
+++ b/solution.py
@@ -8,6 +8,11 @@
 SECTION = 1
 CELLS = ("cells_0", "cells_1", "cells_2")
 plan = (28.0 / 3.0, 7.0, 4.0, 2.0)
+
+
+def tiled_gather(x, axis, dim):
+    copies = jnp.concatenate([x] * lax.axis_size(axis), axis=dim)
+    return lax.all_to_all(copies, axis, dim, dim, tiled=True)
 
 
 def from_everyone(shard, axis):
@@ -101,7 +106,7 @@
     noise = perturbation(member_seeds, positions)
     scaled = (predicted - mean_pred) / (obs_sigma * math.sqrt(members - 1.0))
     innovation = observed / obs_sigma + jnp.sqrt(alpha) * noise - predicted / obs_sigma
-    gathered = lax.all_gather(scaled, "mem", axis=0, tiled=True)
+    gathered = tiled_gather(scaled, "mem", 0)
     gram_matrix, cross_terms = together_2(
         (
             jnp.dot(gathered, gathered.T, precision=highest),

time: 418 us -> 413 us (0.988)
  waiting for transfers between devices: 95.6 us -> 80.7 us
  starting transfers between devices: 7.93 us -> 17.7 us
  matrix products: 41.9 us -> 37.1 us
  local copies, waits for them, and re-layouts: 42.6 us -> 47.3 us
    all_gather x1 -> x0, waiting for transfers between devices: 61.8 us -> none  [shards(): gathered = lax.all_gather(scaled, 'mem', axis=0, tiled=True)]
    all_to_all x0 -> x1, waiting for transfers between devices: none -> 42.5 us  [tiled_gather(): return lax.all_to_all(copies, axis, dim, dim, tiled=True)]
    all_to_all x2 -> x1, blocking collectives: 18 us -> 8.93 us  [from_everyone(): return lax.all_to_all(copies, axis, split_axis=0, concat_axis=0, tiled=True)]
    all_to_all x0 -> x1, local copies, waits for them, and re-layouts: none -> 5.41 us  [tiled_gather(): return lax.all_to_all(copies, axis, dim, dim, tiled=True)]
    all_to_all x0 -> x1, starting transfers between devices: none -> 4.99 us  [tiled_gather(): return lax.all_to_all(copies, axis, dim, dim, tiled=True)]
    all_to_all x1, blocking collectives: 6.85 us -> 11.7 us  [summed_on_arrival(): lax.all_to_all(in_blocks(shard, dim, devices), axis, 0, 0, tiled=True)]
    all_to_all x1 -> x2, starting transfers between devices: 7.89 us -> 12.7 us  [from_everyone(): return lax.all_to_all(copies, axis, split_axis=0, concat_axis=0, tiled=True)]
    all_to_all x1 -> x2, waiting for transfers between devices: 33.7 us -> 38.2 us  [from_everyone(): return lax.all_to_all(copies, axis, split_axis=0, concat_axis=0, tiled=True)]
  transfers between devices with their start and end apart: 3 -> 4, of which waited for: 2 -> 3; matrix products, arithmetic and copies ran while one was open for 42% -> 42% of each run, Pallas kernels for 0% -> 0%
where the time goes in v1:
time: 413 us; the launch traced here: 407 us
  other arithmetic  133 us (32%)
  waiting for transfers between devices  80.7 us (20%)
  blocking collectives  74.8 us (18%)
  local copies, waits for them, and re-layouts  47.3 us (11%)
  matrix products  37.1 us (9%)
  starting transfers between devices  17.7 us (4%)
  between operations  16.8 us (4%)
    another operation x14, other arithmetic, shards(): jnp.linalg.cholesky(gram_matrix + alpha * jnp.eye(members, dtype=jnp.floa...  83.9 us
    all_to_all x1, blocking collectives, summed_rows(): lax.all_to_all(nearer, far, split_axis=0, concat_axis=0, tiled=True)  54.2 us
    all_to_all x1, waiting for transfers between devices, tiled_gather(): return lax.all_to_all(copies, axis, dim, dim, tiled=True)  42.5 us
    another operation x3, other arithmetic, shards(): weights = jax.scipy.linalg.cho_solve((factor, True), cross_terms)  40.3 us
    all_to_all x2, waiting for transfers between devices, from_everyone(): return lax.all_to_all(copies, axis, split_axis=0, concat_axis=0, tiled=True)  38.2 us
    all_to_all x2, starting transfers between devices, from_everyone(): return lax.all_to_all(copies, axis, split_axis=0, concat_axis=0, tiled=True)  12.7 us
    all_to_all x1, blocking collectives, summed_on_arrival(): lax.all_to_all(in_blocks(shard, dim, devices), axis, 0, 0, tiled=True)  11.7 us
    another operation x20, local copies, waits for them, and re-layouts  10.9 us
  transfers between devices with their start and end apart: 4, of which 3 were waited for; matrix products, arithmetic and copies ran while one was open for 42% of the time, Pallas kernels for 0%

profile of v1, /device:TPU:1, one launch (start us, length us, event | category | flops | bytes accessed | tf_op | source)
XLA Modules:
  0.0 407.1 jit_solution(15197538853626586906)
XLA Ops:
  6.5 1.5 copy.73
  8.1 0.7 fusion.75
  8.8 5.5 %gather_fusion = f32[2048,128]{1,0:T(8,128)S(1)} fusion(f32[128,2048]{0,1:T(8,128)S(1)} %copy.73, s32[2048]{0:T(1024)S(1)} %fusion.75), kind=kCustom, calls=%fused_computation | custom fusion | bytes 2105344 | tf_op jit(solution)/shard_map/gather | solution.py:100
  14.7 0.7 broadcast_in_dim.10
  15.4 4.8 %all-to-all-start = ((f32[4,1,4096]{2,1,0:T(1,128)}), f32[4,1,4096]{2,1,0:T(1,128)S(1)}, u32[]{:S(2)}, u32[]{:S(2)}) async-start(f32[4,1,4096]{2,1,0:T(1,128)} %broadcast_in_dim.10), calls=%async_computation | async-start | bytes 131072 | tf_op jit(solution)/shard_map/all_to_all | solution.py:20
  20.2 4.5 %all-to-all-done = f32[4,1,4096]{2,1,0:T(1,128)S(1)} async-done(((f32[4,1,4096]{2,1,0:T(1,128)}), f32[4,1,4096]{2,1,0:T(1,128)S(1)}, u32[]{:S(2)}, u32[]{:S(2)}) %all-to-all-start) | async-done | bytes 65568 | tf_op jit(solution)/shard_map/all_to_all | solution.py:20
  24.8 0.7 divide_bitcast_fusion
  25.5 2.2 copy_bitcast_fusion
  27.7 5.0 %all-to-all-start.1 = ((f32[4,128,2048]{1,2,0:T(8,128)}), f32[4,128,2048]{1,2,0:T(8,128)}, u32[]{:S(2)}, u32[]{:S(2)}) async-start(f32[4,128,2048]{1,2,0:T(8,128)} %copy_bitcast_fusion), calls=%async_computation.1 | async-start | bytes 8388608 | tf_op jit(solution)/shard_map/all_to_all | solution.py:15
  32.8 42.5 %all-to-all-done.1 = f32[4,128,2048]{1,2,0:T(8,128)} async-done(((f32[4,128,2048]{1,2,0:T(8,128)}), f32[4,128,2048]{1,2,0:T(8,128)}, u32[]{:S(2)}, u32[]{:S(2)}) %all-to-all-start.1) | async-done | bytes 4194336 | tf_op jit(solution)/shard_map/all_to_all | solution.py:15
  75.3 5.4 %copy.76 = f32[4,128,2048]{2,1,0:T(8,128)} copy(f32[4,128,2048]{1,2,0:T(8,128)} %all-to-all-done.1) | data formatting | bytes 8388608 | tf_op jit(solution)/shard_map/all_to_all | solution.py:15
  80.7 9.7 %convolution_bitcast_fusion.1 = f32[64,4,8,128]{3,2,1,0:T(8,128)S(1)} fusion(f32[512,2048]{1,0:T(8,128)} %bitcast.82), kind=kOutput, calls=%fused_computation.9 | convolution fusion | flops 6442450944 | bytes 5242880 | tf_op jit(solution)/shard_map/dot_general | solution.py:112
  90.7 7.6 %convolution_bitcast_fusion = f32[65536]{0:T(1024)S(1)} fusion(f32[512,2048]{1,0:T(8,128)S(1)} %bitcast.83, f32[2048,128]{1,0:T(8,128)S(1)} %gather_fusion, f32[2048]{0:T(1024)S(1)} %copy-done.5, s32[128]{0:T(128)S(1)} %get-tuple-element.58, s32[2048]{0:T(1024)S(1)} %add_select_fusion.1, s32[128]{0:T(128)S(1)} %get-tuple-element.57, ...), kind=kOutput, calls=%fused_computation.3 | convolution fusion | flops 1614807040 | bytes 5530624 | tf_op jit(solution)/shard_map/dot_general | solution.py:113
  98.4 1.8 reshape_reshape.4
  100.1 1.6 copy.77
  101.7 11.7 %all_to_all.46 = f32[2,64,2560]{2,1,0:T(8,128)S(1)} all-to-all(f32[2,64,2560]{2,1,0:T(8,128)S(1)} %copy.77), channel_id=1, replica_groups=mesh['cells_0'=16,'cells_1'=4,'cells_2'=2,'mem'=4] {'cells_2'}, dimensions={0} | all-to-all | bytes 2621440 | tf_op jit(solution)/shard_map/all_to_all | solution.py:61
  114.0 54.2 %all_to_all.47 = f32[64,1,2560]{2,1,0:T(1,128)S(1)} all-to-all(f32[64,1,2560]{2,1,0:T(1,128)S(1)} %all_to_all.35), channel_id=1, replica_groups=mesh['cells_0'=16,'cells_1'=4,'cells_2'=2,'mem'=4] {'cells_0','cells_1'}, dimensions={0} | all-to-all | bytes 1310720 | tf_op jit(solution)/shard_map/all_to_all | solution.py:69
  168.6 1.2 broadcast_in_dim.12
  169.8 7.9 %all-to-all-start.4 = ((f32[64,1,2560]{2,1,0:T(1,128)}), f32[64,1,2560]{2,1,0:T(1,128)S(1)}, u32[]{:S(2)}, u32[]{:S(2)}) async-start(f32[64,1,2560]{2,1,0:T(1,128)} %broadcast_in_dim.12), calls=%async_computation.4 | async-start | bytes 1310720 | tf_op jit(solution)/shard_map/all_to_all | solution.py:20
  177.8 1.1 broadcast_subtract_fusion
  178.9 33.7 %all-to-all-done.4 = f32[64,1,2560]{2,1,0:T(1,128)S(1)} async-done(((f32[64,1,2560]{2,1,0:T(1,128)}), f32[64,1,2560]{2,1,0:T(1,128)S(1)}, u32[]{:S(2)}, u32[]{:S(2)}) %all-to-all-start.4) | async-done | bytes 655392 | tf_op jit(solution)/shard_map/all_to_all | solution.py:20
  212.8 8.9 %all_to_all.48 = f32[2,64,2560]{2,1,0:T(8,128)S(1)} all-to-all(f32[2,64,2560]{2,1,0:T(8,128)S(1)} %broadcast_in_dim.24), channel_id=1, replica_groups=mesh['cells_0'=16,'cells_1'=4,'cells_2'=2,'mem'=4] {'cells_2'}, dimensions={0} | all-to-all | bytes 2621440 | tf_op jit(solution)/shard_map/all_to_all | solution.py:20
  221.7 1.0 copy.78
  222.7 2.1 slice.179
  224.8 2.3 slice.197
  227.1 1.6 copy.96
  228.7 1.1 select_add_fusion
  229.8 2.6 copy.80
  232.4 1.4 fusion.8
  233.8 1.0 copy-done.2
  234.8 11.7 %cholesky.103 = f32[128,128]{1,0:T(8,128)S(1)} custom-call(f32[128,128]{1,0:T(8,128)S(1)} %cholesky.263), custom_call_target="Cholesky" | custom-call | tf_op jit(solution)/shard_map/jit(cholesky)/cholesky | solution.py:117
  246.6 9.8 %custom-call.34 = f32[1,128,128]{1,2,0:T(8,128)S(1)} custom-call(f32[1,128,128]{2,1,0:T(8,128)S(1)} %get-tuple-element.52), custom_call_target="InvertDiagBlocksLowerTriangular" | custom-call | tf_op jit(solution)/shard_map/jit(cholesky)/cholesky | solution.py:117
  256.4 1.2 fusion.37
  257.6 1.3 convolution_subtract_fusion
  258.9 11.8 %cholesky.215 = f32[128,128]{1,0:T(8,128)S(1)} custom-call(f32[128,128]{1,0:T(8,128)S(1)} %cholesky.267), custom_call_target="Cholesky" | custom-call | tf_op jit(solution)/shard_map/jit(cholesky)/cholesky | solution.py:117
  270.8 0.6 select_reduce_fusion.2
  271.5 0.8 copy.82
  272.5 10.6 %custom-call.35 = f32[1,128,128]{1,2,0:T(8,128)S(1)} custom-call(f32[1,128,128]{2,1,0:T(8,128)} %get-tuple-element.50), custom_call_target="InvertDiagBlocksLowerTriangular" | custom-call | tf_op jit(solution)/shard_map/jit(cholesky)/cholesky | solution.py:117
  283.2 0.9 constant_dynamic-update-slice_fusion.3
  284.2 1.2 convolution_dynamic-update-slice_fusion
  285.4 1.5 convolution_subtract_fusion.1
  287.5 13.2 %cholesky.236 = f32[128,128]{1,0:T(8,128)} custom-call(f32[128,128]{1,0:T(8,128)} %cholesky.272), custom_call_target="Cholesky" | custom-call | tf_op jit(solution)/shard_map/jit(cholesky)/cholesky | solution.py:117
  300.7 1.5 select_reduce_fusion.1
  302.2 1.6 copy.85
  303.7 2.1 slice.181
  305.8 0.8 constant_dynamic-update-slice_fusion
  306.7 10.6 %custom-call.36 = f32[1,128,128]{1,2,0:T(8,128)S(1)} custom-call(f32[1,128,128]{2,1,0:T(8,128)} %get-tuple-element.48), custom_call_target="InvertDiagBlocksLowerTriangular" | custom-call | tf_op jit(solution)/shard_map/jit(cholesky)/cholesky | solution.py:117
  317.6 1.5 convolution_subtract_fusion.8
  319.2 11.7 %cholesky.253 = f32[128,128]{1,0:T(8,128)S(1)} custom-call(f32[128,128]{1,0:T(8,128)S(1)} %convolution_subtract_fusion.8), custom_call_target="Cholesky" | custom-call | tf_op jit(solution)/shard_map/jit(cholesky)/cholesky | solution.py:117
  331.0 0.7 compare_reduce_fusion.2
  333.0 0.7 compare_reduce_fusion.1
  334.4 0.7 compare_reduce_fusion
  336.0 11.0 %while.1 = (s32[]{:T(128)}, f32[512,512]{0,1:T(8,128)S(1)}, s32[4,2]{0,1:T(2,128)S(1)}, f32[4,128,128]{2,1,0:T(8,128)}, s32[]{:T(128)}) while((s32[]{:T(128)}, f32[512,512]{0,1:T(8,128)S(1)}, s32[4,2]{0,1:T(2,128)S(1)}, f32[4,128,128]{2,1,0:T(8,128)}, s32[]{:T(128)}) %tuple.32), condition=%wide.while_cond, body=%wide.while_body.sunk | while | flops 2 | bytes 393829 | solution.py:118
  336.7 1.3 dynamic-slice.7
  339.4 1.3 dynamic-slice.7
  340.9 0.6 bitcast_dynamic-update-slice_fusion.2
  342.2 1.3 dynamic-slice.7
  344.9 1.3 dynamic-slice.7
  347.0 40.1 %custom-call.37 = f32[4,128,128]{1,2,0:T(8,128)S(1)} custom-call(f32[4,128,128]{2,1,0:T(8,128)} %get-tuple-element.12), custom_call_target="InvertDiagBlocksLowerTriangular" | custom-call | tf_op jit(solution)/shard_map/jit(_cho_solve)/triangular_solve | solution.py:118
  387.1 1.1 fusion.61
  388.2 1.1 convolution_subtract_fusion.5
  389.7 1.2 convolution_subtract_fusion.4
  391.2 1.3 convolution_subtract_fusion.7
  394.5 5.5 %fusion = f32[128,2048]{1,0:T(8,128)} fusion(f32[128,2048]{1,0:T(8,128)S(1)} %copy-done.1, f32[512,2048]{1,0:T(8,128)} %all-gather.2.cloned.1.call-done, f32[128,128]{1,0:T(8,128)S(1)} %fusion.73, f32[128,128]{1,0:T(8,128)S(1)} %fusion.71, f32[128,128]{1,0:T(8,128)S(1)} %fusion.69, f32[128,128]{1,0:T(8,128)S(1)} %fusion.68), kind=kOutput, calls=%fused_computation.7 | convolution fusion | flops 1611333632 | bytes 6553600 | tf_op jit(solution)/shard_map/dot_general | solution.py:120
  (72 shorter events, 11.1 us)
Async XLA Ops:
  8.8 5.8 %copy-start.1 = (f32[128,2048]{1,0:T(8,128)S(1)}, f32[128,2048]{1,0:T(8,128)}, u32[]{:S(2)}) copy-start(f32[128,2048]{1,0:T(8,128)} %param.5) | copy-start | bytes 3145732
  8.8 11.4 %copy-start.4 = (f32[2048]{0:T(1024)S(1)}, f32[2048]{0:T(1024)}, u32[]{:S(2)}) copy-start(f32[2048]{0:T(1024)} %param.6) | copy-start | bytes 24580
  8.8 11.4 %copy-start.5 = (f32[2048]{0:T(1024)S(1)}, f32[2048]{0:T(1024)}, u32[]{:S(2)}) copy-start(f32[2048]{0:T(1024)} %param.7) | copy-start | bytes 24580
  15.4 9.3 %all-to-all-start = ((f32[4,1,4096]{2,1,0:T(1,128)}), f32[4,1,4096]{2,1,0:T(1,128)S(1)}, u32[]{:S(2)}, u32[]{:S(2)}) async-start(f32[4,1,4096]{2,1,0:T(1,128)} %broadcast_in_dim.10), calls=%async_computation | async-start | bytes 131072 | tf_op jit(solution)/shard_map/all_to_all | solution.py:20
  27.7 5.0 %copy-start.6 = (s32[128]{0:T(128)S(1)}, s32[128]{0:T(128)}, u32[]{:S(2)}) copy-start(s32[128]{0:T(128)} %param.9) | copy-start | bytes 1540
  27.7 47.5 %all-to-all-start.1 = ((f32[4,128,2048]{1,2,0:T(8,128)}), f32[4,128,2048]{1,2,0:T(8,128)}, u32[]{:S(2)}, u32[]{:S(2)}) async-start(f32[4,128,2048]{1,2,0:T(8,128)} %copy_bitcast_fusion), calls=%async_computation.1 | async-start | bytes 8388608 | tf_op jit(solution)/shard_map/all_to_all | solution.py:15
  80.7 10.0 %copy-start = (f32[4,128,2048]{2,1,0:T(8,128)S(1)}, f32[4,128,2048]{2,1,0:T(8,128)}, u32[]{:S(2)}) copy-start(f32[4,128,2048]{2,1,0:T(8,128)} %copy.76) | copy-start | bytes 12582916
  169.8 42.8 %all-to-all-start.4 = ((f32[64,1,2560]{2,1,0:T(1,128)}), f32[64,1,2560]{2,1,0:T(1,128)S(1)}, u32[]{:S(2)}, u32[]{:S(2)}) async-start(f32[64,1,2560]{2,1,0:T(1,128)} %broadcast_in_dim.12), calls=%async_computation.4 | async-start | bytes 1310720 | tf_op jit(solution)/shard_map/all_to_all | solution.py:20
  177.7 216.8 %all-gather.2.cloned.1.call-start = ((), (), s32[]{:S(2)}) async-start(), calls=%async_computation.6 | async-start | bytes 5242880 | tf_op jit(solution)/shard_map/all_gather | solution.py:121
  233.8 1.0 copy-start.2
  258.9 13.4 %copy-start.3 = (f32[384,128]{1,0:T(8,128)}, f32[384,128]{1,0:T(8,128)S(1)}, u32[]{:S(2)}) copy-start(f32[384,128]{1,0:T(8,128)S(1)} %convolution_subtract_fusion) | copy-start | bytes 589828
Sparse Core Ops, SparseCore 0:
  180.6 55.3 all-gather.1
